TPU v7x, 256 devices: a whole 4x4x8 slice. The times are simulated.
256 devices in a mesh: row: 16 (over z_lo, x), col: 16 (over y, z_hi, core).
Axes of the slice: x: 4, y: 4, z: 8 (z_hi: 2, z_lo: 4; z = z_hi * 4 + z_lo), core: 2. Of those that a mesh axis runs over, the one named last changes fastest.
Arguments:
- homolog_matrix: bfloat16 [128, 1280, 64], P('row', 'col'), may hold values from -6 to 6
- contact_matrix: bfloat16 [1280, 1280, 128], P('row', 'col'), may hold values from -24 to 24
- genuine_homolog_total: int32 [1], replicated, may hold values from 1 to 128
- genuine_chain_length: int32 [1], replicated, may hold values from 640 to 1280
- tensor_product_matrices: bfloat16 [1, 64, 64], replicated, may hold values from -0.75 to 0.75
- tensor_product_final: bfloat16 [1, 1024, 128], replicated, may hold values from -0.75 to 0.75
- mixing_value_gate_matrix: bfloat16 [1, 64, 512], replicated, may hold values from -0.75 to 0.75
- mixing_logit_matrix: bfloat16 [1, 128, 8], replicated
- mixing_final_matrix: bfloat16 [1, 256, 64], replicated, may hold values from -1.5 to 1.5
- feedforward_gate_expand: bfloat16 [1, 128, 1024], replicated, may hold values from -0.5 to 0.5
- feedforward_shrink_matrix: bfloat16 [1, 512, 128], replicated, may hold values from -0.25 to 0.25
Outputs:
- msa_out: bfloat16 [128, 1280, 64], P('row', 'col')
- pair_out: bfloat16 [1280, 1280, 128], P('row', 'col')
Inputs may be any that keep to these rules, and one draw needn't show every extreme that they name: Sequences from genuine_homolog_total on are padding. Residues from genuine_chain_length on are padding.
All inputs are finite; a program needn't handle non-finite values.
Results may differ from a plain program's by a relative error of at most 0.0065.
The roundings to bfloat16 on the way count: a program that leaves them out, or rounds other values in their place, can miss the bound.
Values may be sent and summed in bfloat16 or wider, within the bound.
No kernel may reach another device: no remote copies, remote signals or barrier semaphores. Data moves between devices by JAX's collectives and lax.ppermute only.
A program may use at most 64 MiB of HBM per device.

v0:
```python
import jax
import jax.numpy as jnp
from jax import lax
from jax.sharding import PartitionSpec as P

EPSILON = 1e-05
MASKED = -1000000000.0


def in_order(parts, dim):
    parts = jnp.moveaxis(parts, 0, dim)
    lengths = parts.shape
    return parts.reshape(*lengths[:dim], lengths[dim] * lengths[dim + 1], *lengths[dim + 2 :])


def from_everyone(value, axis):
    count = lax.axis_size(axis)
    return lax.all_to_all(
        jnp.broadcast_to(value[None], (count, *value.shape)), axis, 0, 0, tiled=True
    )


def gather_directly(value, axis, dim):
    return in_order(from_everyone(value, axis), dim)


def picked(value, axis, root):
    return lax.dynamic_index_in_dim(lax.all_gather(value, axis), root, 0, keepdims=False)


def of_everyone(value, axis):
    everything = from_everyone(value, axis)
    return jnp.max(everything, axis=0)


def over_copies(value, axis):
    return from_everyone(value, axis).sum(axis=0)


def standardize_features(field):
    field = field.astype(jnp.float32)
    center = field - jnp.mean(field, axis=-1, keepdims=True)
    spread = jnp.mean(center * center, axis=-1, keepdims=True)
    return center * lax.rsqrt(spread + EPSILON)


def local(
    homolog_matrix,
    contact_matrix,
    genuine_homolog_total,
    genuine_chain_length,
    tensor_product_matrices,
    tensor_product_final,
    mixing_value_gate_matrix,
    mixing_logit_matrix,
    mixing_final_matrix,
    feedforward_gate_expand,
    feedforward_shrink_matrix,
):
    homolog_rows_local, chain_positions_local, homolog_rows_full = homolog_matrix.shape
    rows_dev = contact_matrix.shape[0]
    pair_width = contact_matrix.shape[2]
    outer_width = tensor_product_matrices.shape[2] // 2
    head_count = mixing_logit_matrix.shape[2]
    hidden_width = mixing_final_matrix.shape[1]
    head_width = hidden_width // head_count
    trans_width = feedforward_shrink_matrix.shape[1]
    row_blocks = rows_dev // 8
    row_index = lax.axis_index("row")
    col_index = lax.axis_index("col")
    ratio = lax.axis_size("row") // lax.axis_size("col")
    total_seqs = homolog_rows_local * lax.axis_size("row")
    seq_ids = row_index * homolog_rows_local + jnp.arange(homolog_rows_local, dtype=jnp.int32)
    res_ids = col_index * chain_positions_local + jnp.arange(chain_positions_local, dtype=jnp.int32)
    pair_ids = row_index * rows_dev + jnp.arange(rows_dev, dtype=jnp.int32)
    seq_float = (seq_ids < genuine_homolog_total[0]).astype(jnp.float32)
    res_valid = res_ids < genuine_chain_length[0]
    res_float = res_valid.astype(jnp.float32)
    row_float = (pair_ids < genuine_chain_length[0]).astype(jnp.float32)
    divisor = jnp.maximum(
        genuine_homolog_total[0].astype(jnp.float32) * row_float[:, None] * res_float[None, :], 1.0
    )
    starts = jnp.arange(row_blocks, dtype=jnp.int32) * 8
    standardized_source = standardize_features(homolog_matrix).astype(jnp.bfloat16)
    reshaped_tensor = standardized_source.reshape(
        homolog_rows_local * chain_positions_local, homolog_rows_full
    )
    projected = jnp.dot(
        reshaped_tensor, tensor_product_matrices[0], preferred_element_type=jnp.float32
    ).reshape(homolog_rows_local, chain_positions_local, 2 * outer_width)
    projected = (projected * (seq_float[:, None, None] * res_float[None, :, None])).astype(
        jnp.bfloat16
    )
    packed = projected.reshape(homolog_rows_local, chain_positions_local * 2 * outer_width)
    columns = gather_directly(packed, "row", 0).reshape(
        total_seqs, chain_positions_local, 2 * outer_width
    )
    left_all = columns[:, :, :outer_width].reshape(total_seqs, chain_positions_local * outer_width)
    right = columns[:, :, outer_width:].reshape(total_seqs, chain_positions_local * outer_width)
    left_cols = picked(left_all, "col", row_index // ratio).reshape(
        total_seqs, chain_positions_local, outer_width
    )
    outer_weight = tensor_product_final[0]

    def outer_rows(inputs):
        start, pair_rows = inputs
        rows = lax.dynamic_slice_in_dim(left_cols, start, 8, 1).reshape(total_seqs, 8 * outer_width)
        product = lax.dot_general(
            rows, right, (((0,), (0,)), ((), ())), preferred_element_type=jnp.float32
        )
        product = product.reshape(8, outer_width, chain_positions_local, outer_width).transpose(
            0, 2, 1, 3
        )
        product = product.reshape(8, chain_positions_local, outer_width * outer_width)
        scale = lax.dynamic_slice_in_dim(divisor, start, 8, 0)
        outer = (product / scale[:, :, None]).astype(jnp.bfloat16)
        update = jnp.dot(
            outer.reshape(8 * chain_positions_local, outer_width * outer_width),
            outer_weight,
            preferred_element_type=jnp.float32,
        )
        return (
            pair_rows.astype(jnp.float32) + update.reshape(8, chain_positions_local, pair_width)
        ).astype(jnp.bfloat16)

    contact_matrix = lax.map(
        outer_rows,
        (starts, contact_matrix.reshape(row_blocks, 8, chain_positions_local, pair_width)),
    ).reshape(rows_dev, chain_positions_local, pair_width)
    bias_weight = mixing_logit_matrix[0]

    def norm_rows(pair_rows):
        normed_rows = standardize_features(pair_rows).astype(jnp.bfloat16)
        logit_rows = jnp.dot(
            normed_rows.reshape(8 * chain_positions_local, pair_width),
            bias_weight,
            preferred_element_type=jnp.float32,
        )
        return (normed_rows, logit_rows.reshape(8, chain_positions_local, head_count))

    pair_normed, logits = lax.map(
        norm_rows, contact_matrix.reshape(row_blocks, 8, chain_positions_local, pair_width)
    )
    logits = jnp.where(
        res_valid[None, :, None],
        logits.reshape(rows_dev, chain_positions_local, head_count),
        MASKED,
    )
    logits = logits.transpose(0, 2, 1)
    peak = of_everyone(jnp.max(logits, axis=2), "col")
    expo = jnp.exp(logits - peak[:, :, None])
    totals = over_copies(jnp.sum(expo, axis=2), "col")
    local_weights = (expo / totals[:, :, None]).astype(jnp.bfloat16)
    part_rows = rows_dev // lax.axis_size("row")
    sectioned = local_weights.reshape(1, rows_dev, head_count, 1, chain_positions_local)
    moved = lax.all_to_all(
        lax.all_to_all(sectioned, "row", split_axis=1, concat_axis=0, tiled=True),
        "col",
        split_axis=0,
        concat_axis=3,
        tiled=True,
    )
    moved = moved.reshape(
        ratio, part_rows, head_count, lax.axis_size("col") * chain_positions_local
    )
    mine = gather_directly(moved, "row", 1).reshape(
        chain_positions_local, head_count, lax.axis_size("col") * chain_positions_local
    )
    value_weight = mixing_value_gate_matrix[0][:, :hidden_width]
    gate_weight = mixing_value_gate_matrix[0][:, hidden_width:]
    gate = jax.nn.sigmoid(
        jnp.dot(reshaped_tensor, gate_weight, preferred_element_type=jnp.float32)
    ).reshape(homolog_rows_local, chain_positions_local, hidden_width)
    values_local = jnp.dot(reshaped_tensor, value_weight, preferred_element_type=jnp.float32)
    values_local = values_local.astype(jnp.bfloat16).reshape(
        homolog_rows_local, chain_positions_local, hidden_width
    )
    values_piece = lax.all_gather(values_local, "col", axis=1, tiled=True)
    count = values_piece.shape[1]
    heads_piece = values_piece.reshape(homolog_rows_local, count, head_count, head_width)
    averaged = jnp.einsum("ihj,sjhc->sihc", mine, heads_piece, preferred_element_type=jnp.float32)
    gated = (
        gate * averaged.reshape(homolog_rows_local, chain_positions_local, hidden_width)
    ).astype(jnp.bfloat16)
    contact_increment = jnp.dot(
        gated.reshape(homolog_rows_local * chain_positions_local, hidden_width),
        mixing_final_matrix[0],
        preferred_element_type=jnp.float32,
    )
    homolog_matrix = (
        homolog_matrix.astype(jnp.float32)
        + contact_increment.reshape(homolog_rows_local, chain_positions_local, homolog_rows_full)
    ).astype(jnp.bfloat16)
    up_weight = feedforward_gate_expand[0]
    down_weight = feedforward_shrink_matrix[0]

    def transition_rows(inputs):
        pair_rows, normed_rows = inputs
        hidden = jnp.dot(
            normed_rows.reshape(8 * chain_positions_local, pair_width),
            up_weight,
            preferred_element_type=jnp.float32,
        )
        active = (jax.nn.silu(hidden[:, :trans_width]) * hidden[:, trans_width:]).astype(
            jnp.bfloat16
        )
        update = jnp.dot(active, down_weight, preferred_element_type=jnp.float32)
        return (
            pair_rows.astype(jnp.float32) + update.reshape(8, chain_positions_local, pair_width)
        ).astype(jnp.bfloat16)

    contact_matrix = lax.map(
        transition_rows,
        (contact_matrix.reshape(row_blocks, 8, chain_positions_local, pair_width), pair_normed),
    )
    contact_matrix = contact_matrix.reshape(rows_dev, chain_positions_local, pair_width)
    return (homolog_matrix, contact_matrix)


def solution(mesh):
    in_specs = (
        P("row", "col", None),
        P("row", "col", None),
        P(),
        P(),
        P(),
        P(),
        P(),
        P(),
        P(),
        P(),
        P(),
    )
    out_specs = (P("row", "col", None), P("row", "col", None))
    return jax.shard_map(local, mesh=mesh, in_specs=in_specs, out_specs=out_specs, check_vma=False)
```

profile of v0, /device:TPU:32, one launch (start us, length us, event | category | flops | bytes accessed | tf_op | source)
XLA Modules:
  0.0 403.6 jit_solution(8511673040539516351)
XLA Ops:
  8.5 0.9 convert_reduce_fusion.1
  9.5 1.0 fusion.45
  10.5 0.9 fusion.46
  11.5 0.9 fusion.39
  12.9 40.2 %all_to_all.47 = bf16[16,8,5120]{2,1,0:T(8,128)(2,1)} all-to-all(bf16[16,8,5120]{2,1,0:T(8,128)(2,1)S(1)} %broadcast_in_dim.40), channel_id=1, replica_groups=mesh['row'=16,'col'=16] {'row'}, dimensions={0} | all-to-all | bytes 2621440 | tf_op jit(solution)/shard_map/all_to_all | solution.py:18
  53.1 3.3 reshape_reshape.3
  56.4 3.2 fusion.53
  59.7 4.4 %copy.88 = bf16[128,80,32]{0,2,1:T(8,128)(2,1)S(1)} copy(bf16[128,80,32]{2,1,0:T(8,128)(2,1)} %get-tuple-element.149) | data formatting | bytes 1310720 | tf_op jit(solution)/shard_map/slice | solution.py:98
  64.1 1.1 copy.89
  67.0 3.6 copy.91
  70.6 117.3 %all-gather.5.cloned.1.call-done = bf16[16,128,2560]{2,1,0:T(8,128)(2,1)} async-done(((bf16[1,128,2560]{2,1,0:T(8,128)(2,1)}), bf16[16,128,2560]{2,1,0:T(8,128)(2,1)}) %all-gather.5.cloned.1.call-update) | async-done | bytes 10485776 | tf_op jit(solution)/shard_map/all_gather | solution.py:28
  188.0 1.1 constant_dynamic-slice_fusion.2
  190.0 77.5 %while.32 = (s32[]{:T(128)}, bf16[10,8,80,128]{3,2,1,0:T(8,128)(2,1)S(1)}, bf16[10,8,80,128]{3,2,1,0:T(8,128)(2,1)}, s32[10]{0:T(128)S(1)}, bf16[128,80,32]{0,2,...) while((s32[]{:T(128)}, ...), condition=%wide.region_3.4_spmd, body=%wide.region_2.3_spmd.sunk | while | flops 337100800 | bytes 15212199 | solution.py:126
  193.3 2.4 copy.125
  196.1 1.7 fusion.86
  201.1 2.4 copy.125
  203.8 1.7 fusion.86
  208.8 2.4 copy.125
  211.6 1.7 fusion.86
  216.6 2.4 copy.125
  219.3 1.7 fusion.86
  224.3 2.4 copy.125
  227.1 1.7 fusion.86
  232.1 2.4 copy.125
  234.8 1.7 fusion.86
  239.8 2.4 copy.125
  242.6 1.7 fusion.86
  247.6 2.4 copy.125
  250.3 1.7 fusion.86
  255.3 2.4 copy.125
  258.1 1.7 fusion.86
  263.1 2.4 copy.125
  265.8 1.7 fusion.86
  267.6 1.4 broadcast.151.clone
  269.1 17.8 %while.33 = (s32[]{:T(128)}, bf16[10,8,80,128]{3,2,1,0:T(8,128)(2,1)}, f32[10,8,80,8]{2,3,1,0:T(8,128)S(1)}, bf16[10,8,80,128]{3,2,1,0:T(8,128)(2,1)S(1)}, bf16[128,8]{0,1:T(8,128)(2,1)S(1)}, /*index=5*/s32[]{:T(128)}) while((s32[]{:T(128)}, bf16[10,8,80,128]{3,2,1,0:T(8,128)(2,1)}, f32[10,8,80,8]{2,3,1,0:T(8,128)S(1)}, ...), condition=%wide.region_7.8_spmd, body=%wide.region_4.7_spmd.sunk | while | flops 2458242 | bytes 886861 | solution.py:141
  285.6 0.9 fusion.90
  287.1 13.0 %all_to_all.48 = f32[16,80,8]{1,2,0:T(8,128)S(1)} all-to-all(f32[16,80,8]{1,2,0:T(8,128)S(1)} %broadcast_in_dim.66), channel_id=1, replica_groups=mesh['row'=16,'col'=16] {'col'}, dimensions={0} | all-to-all | bytes 81920 | tf_op jit(solution)/shard_map/all_to_all | solution.py:18
  300.6 12.6 %all_to_all.49 = f32[16,80,8]{1,2,0:T(8,128)S(1)} all-to-all(f32[16,80,8]{1,2,0:T(8,128)S(1)} %broadcast_in_dim.67), channel_id=1, replica_groups=mesh['row'=16,'col'=16] {'col'}, dimensions={0} | all-to-all | bytes 81920 | tf_op jit(solution)/shard_map/all_to_all | solution.py:18
  313.6 15.2 %all_to_all.50 = bf16[1,80,8,1,80]{4,2,3,0,1:T(8,128)(2,1)} all-to-all(bf16[1,80,8,1,80]{4,2,3,0,1:T(8,128)(2,1)S(1)} %fusion.47), channel_id=1, replica_groups=mesh['row'=16,'col'=16] {'row'}, dimensions={1} | all-to-all | bytes 204800 | tf_op jit(solution)/shard_map/all_to_all | solution.py:157
  328.8 3.5 all-to-all-start.4
  332.3 8.6 %copy.85 = bf16[8,1280,256]{1,2,0:T(8,128)(2,1)} copy(bf16[8,1280,256]{2,0,1:T(8,128)(2,1)} %all-gather.3.cloned.1.call-done) | data formatting | bytes 10485760 | tf_op jit(solution)/shard_map/all_gather | solution.py:178
  341.0 4.0 all-to-all-done.4
  345.2 1.3 broadcast_in_dim.69
  346.5 4.4 %all-to-all-start.5 = ((bf16[16,1,5,8,1280]{4,3,2,1,0:T(8,128)(2,1)}), bf16[16,1,5,8,1280]{4,3,2,1,0:T(8,128)(2,1)}, u32[]{:S(2)}, u32[]{:S(2)}) async-start(bf16[16,1,5,8,1280]{4,3,2,1,0:T(8,128)(2,1)} %broadcast_in_dim.69), calls=%async_computation.5 | async-start | bytes 3276800 | tf_op jit(solution)/shard_map/all_to_all | solution.py:18
  351.0 1.4 broadcast.151
  352.4 26.3 %while.34 = (s32[]{:T(128)}, bf16[10,8,80,128]{3,2,1,0:T(8,128)(2,1)}, bf16[10,8,80,128]{3,2,1,0:T(8,128)(2,1)S(1)}, bf16[10,8,80,128]{3,2,1,0:T(8,128)(2,1)}, b...) while((s32[]{:T(128)}, bf16[10,8,80,128]{3,2,1,0:T(8,128)(2,1)}, ...), condition=%wide.region_13.14_spmd, body=%wide.region_12.13_spmd.sunk | while | flops 253870080 | bytes 7111249 | solution.py:212
  378.7 10.6 %all-to-all-done.5 = bf16[16,1,5,8,1280]{4,3,2,1,0:T(8,128)(2,1)} async-done(((bf16[16,1,5,8,1280]{4,3,2,1,0:T(8,128)(2,1)}), bf16[16,1,5,8,1280]{4,3,2,1,0:T(8,128)(2,1)}, u32[]{:S(2)}, u32[]{:S(2)}) %all-to-all-start.5) | async-done | bytes 1638432 | tf_op jit(solution)/shard_map/all_to_all | solution.py:18
  389.2 4.5 %fusion.29 = f32[8,80,8,32]{1,3,0,2:T(8,128)S(1)} fusion(bf16[80,8,1280,1]{2,1,0,3:T(8,128)(2,1)} %bitcast.41, bf16[8,1280,8,32]{1,3,2,0:T(8,128)(2,1)} %bitcast.170), kind=kOutput, calls=%fused_computation.40 | convolution fusion | flops 419430400 | bytes 7536640 | tf_op jit(solution)/shard_map/ihj,sjhc->sihc/dot_general | solution.py:181
  (198 shorter events, 67.1 us)
Async XLA Ops:
  7.2 388.1 %copy-start = (bf16[1,256,64]{1,2,0:T(8,128)(2,1)S(1)}, bf16[1,256,64]{1,2,0:T(8,128)(2,1)}, u32[]{:S(2)}) copy-start(bf16[1,256,64]{1,2,0:T(8,128)(2,1)} %param.25) | copy-start | bytes 98308
  7.2 180.8 %all-gather.5.cloned.1.call-start = ((), (), s32[]{:S(2)}) async-start(), calls=%async_computation.7 | async-start | bytes 11141120 | tf_op jit(solution)/shard_map/all_gather | solution.py:28
  64.0 1.4 copy-start.6
  65.1 1.9 copy-start.1
  65.2 267.2 %all-gather.3.cloned.1.call-start = ((), (), s32[]{:S(2)}) async-start(), calls=%async_computation.6 | async-start | bytes 5570560 | tf_op jit(solution)/shard_map/all_gather | solution.py:178
  189.1 1.0 copy-start.2
  267.6 1.5 copy-start.4
  267.6 1.5 copy-start.8
  328.8 16.2 %all-to-all-start.4 = ((bf16[16,5,8,1,80]{4,2,1,3,0:T(8,128)(2,1)}), bf16[16,5,8,1,80]{4,2,1,3,0:T(8,128)(2,1)S(1)}, u32[]{:S(2)}, u32[]{:S(2)}) async-start(bf16[16,5,8,1,80]{4,2,1,3,0:T(8,128)(2,1)} %bitcast.37), calls=%async_computation.4 | async-start | bytes 327680 | tf_op jit(solution)/shard_map/all_to_all | solution.py:156
  346.5 42.7 %all-to-all-start.5 = ((bf16[16,1,5,8,1280]{4,3,2,1,0:T(8,128)(2,1)}), bf16[16,1,5,8,1280]{4,3,2,1,0:T(8,128)(2,1)}, u32[]{:S(2)}, u32[]{:S(2)}) async-start(bf16[16,1,5,8,1280]{4,3,2,1,0:T(8,128)(2,1)} %broadcast_in_dim.69), calls=%async_computation.5 | async-start | bytes 3276800 | tf_op jit(solution)/shard_map/all_to_all | solution.py:18
  351.0 1.4 copy-start.3
  351.0 1.4 copy-start.7
  394.9 0.9 copy-start.5
Sparse Core Ops, SparseCore 0:
  65.3 122.6 all-gather.4
  190.6 79.4 all-gather.2
where the time goes:
time: 405 us; the launch traced here: 404 us
  waiting for transfers between devices  132 us (33%)
  blocking collectives  81.1 us (20%)
  local copies, waits for them, and re-layouts  73.5 us (18%)
  matrix products  44.7 us (11%)
  other arithmetic  28.4 us (7%)
  loops' own time  20.3 us (5%)
  between operations  15.7 us (4%)
  starting transfers between devices  8.03 us (2%)
    all_gather x1, waiting for transfers between devices, picked(): lax.all_gather(value, axis)  117 us
    all_to_all x3, blocking collectives, from_everyone(): lax.all_to_all(jnp.broadcast_to(value[None], (count, *value.shape)), axis...  65.9 us
    transpose x10, local copies, waits for them, and re-layouts, outer_rows(): product.reshape(8, outer_width, chain_positions_local, outer_width)  23.8 us
    another operation x1, loops' own time, local(): lax.map(outer_rows, (starts, contact_matrix.reshape(row_blocks, 8, chain_...  19.9 us
    dot_general x10, matrix products, outer_rows(): jnp.dot(outer.reshape(8 * chain_positions_local, outer_width * outer_widt...  17.1 us
    dynamic_update_slice x20, other arithmetic, local(): lax.map(outer_rows, (starts, contact_matrix.reshape(row_blocks, 8, chain_...  16.3 us
    all_to_all x1, blocking collectives, local(): lax.all_to_all(sectioned, 'row', split_axis=1, concat_axis=0, tiled=True)  15.2 us
    dynamic_slice x20, local copies, waits for them, and re-layouts, local(): lax.map(outer_rows, (starts, contact_matrix.reshape(row_blocks, 8, chain_...  15.1 us
  transfers between devices with their start and end apart: 4, of which 3 were waited for; matrix products, arithmetic and copies ran while one was open for 30% of the time, Pallas kernels for 0%

commit v1 on v0

--- a/solution.py
+++ b/solution.py
@@ -175,7 +175,10 @@
     values_local = values_local.astype(jnp.bfloat16).reshape(
         homolog_rows_local, chain_positions_local, hidden_width
     )
-    values_piece = lax.all_gather(values_local, "col", axis=1, tiled=True)
+    devices = lax.axis_size("col")
+    tiles = jnp.stack([values_local for _ in range(devices)])
+    tiles = lax.all_to_all(tiles, "col", split_axis=0, concat_axis=0)
+    values_piece = jnp.concatenate(tiles, axis=1)
     count = values_piece.shape[1]
     heads_piece = values_piece.reshape(homolog_rows_local, count, head_count, head_width)
     averaged = jnp.einsum("ihj,sjhc->sihc", mine, heads_piece, preferred_element_type=jnp.float32)

time: 405 us -> 554 us (1.37)
  waiting for transfers between devices: 132 us -> 266 us
  blocking collectives: 81.1 us -> 57.7 us
  local copies, waits for them, and re-layouts: 73.5 us -> 93.4 us
  starting transfers between devices: 8.03 us -> 25 us
    all_to_all x0 -> x1, waiting for transfers between devices: none -> 117 us  [local(): tiles = lax.all_to_all(tiles, 'col', split_axis=0, concat_axis=0)]
    all_to_all x3 -> x1, blocking collectives: 65.9 us -> 40.2 us  [from_everyone(): lax.all_to_all(jnp.broadcast_to(value[None], (count, *value.shape)), axis...]
    all_to_all x1 -> x3, waiting for transfers between devices: 10.6 us -> 30.3 us  [from_everyone(): lax.all_to_all(jnp.broadcast_to(value[None], (count, *value.shape)), axis...]
    another operation x3 -> x5, local copies, waits for them, and re-layouts: 3.12 us -> 19.9 us  [the longest x1 14 us: local(): values_piece.reshape(homolog_rows_local, count, head_count, head_width)]
    reshape x1, local copies, waits for them, and re-layouts: 0.83 us -> 11.4 us  [local(): values_piece = jnp.concatenate(tiles, axis=1)]
    all_to_all x1 -> x3, starting transfers between devices: 4.43 us -> 13.3 us  [from_everyone(): lax.all_to_all(jnp.broadcast_to(value[None], (count, *value.shape)), axis...]
    all_gather x1 -> x0, local copies, waits for them, and re-layouts: 8.63 us -> none  [local(): values_piece = lax.all_gather(values_local, 'col', axis=1, tiled=True)]
  transfers between devices with their start and end apart: 4 -> 6, of which waited for: 3 -> 5; matrix products, arithmetic and copies ran while one was open for 30% -> 10% of each run, Pallas kernels for 0% -> 0%
where the time goes in v1:
time: 554 us; the launch traced here: 551 us
  waiting for transfers between devices  266 us (48%)
  local copies, waits for them, and re-layouts  93.4 us (17%)
  blocking collectives  57.7 us (10%)
  matrix products  44.7 us (8%)
  other arithmetic  28.2 us (5%)
  starting transfers between devices  25 us (5%)
  loops' own time  20.3 us (4%)
  between operations  15.7 us (3%)
    all_gather x1, waiting for transfers between devices, picked(): lax.all_gather(value, axis)  119 us
    all_to_all x1, waiting for transfers between devices, local(): tiles = lax.all_to_all(tiles, 'col', split_axis=0, concat_axis=0)  117 us
    all_to_all x1, blocking collectives, from_everyone(): lax.all_to_all(jnp.broadcast_to(value[None], (count, *value.shape)), axis...  40.2 us
    all_to_all x3, waiting for transfers between devices, from_everyone(): lax.all_to_all(jnp.broadcast_to(value[None], (count, *value.shape)), axis...  30.3 us
    transpose x10, local copies, waits for them, and re-layouts, outer_rows(): product.reshape(8, outer_width, chain_positions_local, outer_width)  23.8 us
    another operation x1, loops' own time, local(): lax.map(outer_rows, (starts, contact_matrix.reshape(row_blocks, 8, chain_...  19.9 us
    all_to_all x1, blocking collectives, local(): lax.all_to_all(sectioned, 'row', split_axis=1, concat_axis=0, tiled=True)  17.5 us
    dot_general x10, matrix products, outer_rows(): jnp.dot(outer.reshape(8 * chain_positions_local, outer_width * outer_widt...  17 us
  transfers between devices with their start and end apart: 6, of which 5 were waited for; matrix products, arithmetic and copies ran while one was open for 10% of the time, Pallas kernels for 0%

profile of v1, /device:TPU:32, one launch (start us, length us, event | category | flops | bytes accessed | tf_op | source)
XLA Modules:
  0.0 551.3 jit_solution(18102811643343637259)
XLA Ops:
  12.9 40.2 %all_to_all.52 = bf16[16,8,5120]{2,1,0:T(8,128)(2,1)} all-to-all(bf16[16,8,5120]{2,1,0:T(8,128)(2,1)S(1)} %broadcast_in_dim.40), channel_id=1, replica_groups=mesh['row'=16,'col'=16] {'row'}, dimensions={0} | all-to-all | bytes 2621440 | tf_op jit(solution)/shard_map/all_to_all | solution.py:18
  53.1 3.3 reshape_reshape.7
  56.4 3.3 fusion.53
  59.7 4.5 copy.85
  64.2 1.1 copy.86
  65.5 3.6 copy.88
  69.1 119.0 %all-gather.2.cloned.1.call-done = bf16[16,128,2560]{2,1,0:T(8,128)(2,1)} async-done(((bf16[1,128,2560]{2,1,0:T(8,128)(2,1)}), bf16[16,128,2560]{2,1,0:T(8,128)(2,1)}) %all-gather.2.cloned.1.call-update) | async-done | bytes 10485776 | tf_op jit(solution)/shard_map/all_gather | solution.py:28
  188.1 1.1 constant_dynamic-slice_fusion.2
  190.2 77.5 %while.32 = (s32[]{:T(128)}, bf16[10,8,80,128]{3,2,1,0:T(8,128)(2,1)S(1)}, bf16[10,8,80,128]{3,2,1,0:T(8,128)(2,1)}, s32[10]{0:T(128)S(1)}, bf16[128,80,32]{0,2,...) while((s32[]{:T(128)}, ...), condition=%wide.region_3.4_spmd, body=%wide.region_2.3_spmd.sunk | while | flops 337100800 | bytes 15212207 | solution.py:126
  193.5 2.4 copy.122
  196.2 1.7 fusion.86
  201.3 2.4 copy.122
  204.0 1.7 fusion.86
  209.0 2.4 copy.122
  211.7 1.7 fusion.86
  216.8 2.4 copy.122
  219.5 1.7 fusion.86
  224.5 2.4 copy.122
  227.2 1.7 fusion.86
  232.2 2.4 copy.122
  235.0 1.7 fusion.86
  240.0 2.4 copy.122
  242.7 1.7 fusion.86
  247.7 2.4 copy.122
  250.5 1.7 fusion.86
  255.5 2.4 copy.122
  258.2 1.7 fusion.86
  263.2 2.4 copy.122
  266.0 1.7 fusion.86
  267.7 1.4 broadcast.152.clone
  269.1 17.7 %while.33 = (s32[]{:T(128)}, bf16[10,8,80,128]{3,2,1,0:T(8,128)(2,1)}, f32[10,8,80,8]{2,3,1,0:T(8,128)S(1)}, bf16[10,8,80,128]{3,2,1,0:T(8,128)(2,1)S(1)}, bf16[128,8]{0,1:T(8,128)(2,1)S(1)}, /*index=5*/s32[]{:T(128)}) while((s32[]{:T(128)}, bf16[10,8,80,128]{3,2,1,0:T(8,128)(2,1)}, f32[10,8,80,8]{2,3,1,0:T(8,128)S(1)}, ...), condition=%wide.region_7.8_spmd, body=%wide.region_4.7_spmd.sunk | while | flops 2458242 | bytes 886361 | solution.py:141
  287.7 3.5 all-to-all-start.2
  291.5 9.8 %all-to-all-done.2 = f32[16,80,8]{1,2,0:T(8,128)S(1)} async-done(((f32[16,80,8]{1,2,0:T(8,128)}), f32[16,80,8]{1,2,0:T(8,128)S(1)}, u32[]{:S(2)}, u32[]{:S(2)}) %all-to-all-start.2) | async-done | bytes 40992 | tf_op jit(solution)/shard_map/all_to_all | solution.py:18
  302.3 3.7 all-to-all-start.3
  306.3 9.7 %all-to-all-done.3 = f32[16,80,8]{1,2,0:T(8,128)S(1)} async-done(((f32[16,80,8]{1,2,0:T(8,128)}), f32[16,80,8]{1,2,0:T(8,128)S(1)}, u32[]{:S(2)}, u32[]{:S(2)}) %all-to-all-start.3) | async-done | bytes 40992 | tf_op jit(solution)/shard_map/all_to_all | solution.py:18
  316.0 2.8 stack.3
  318.8 4.6 all-to-all-start
  323.8 117.0 %all-to-all-done = bf16[16,8,80,256]{3,2,1,0:T(8,128)(2,1)} async-done(((bf16[16,8,80,256]{3,2,1,0:T(8,128)(2,1)}), bf16[16,8,80,256]{3,2,1,0:T(8,128)(2,1)}, u32[]{:S(2)}, u32[]{:S(2)}) %all-to-all-start) | async-done | bytes 5242912 | tf_op jit(solution)/shard_map/all_to_all | solution.py:180
  440.8 17.5 %all_to_all.53 = bf16[1,80,8,1,80]{4,2,3,0,1:T(8,128)(2,1)} all-to-all(bf16[1,80,8,1,80]{4,2,3,0,1:T(8,128)(2,1)S(1)} %fusion.47), channel_id=1, replica_groups=mesh['row'=16,'col'=16] {'row'}, dimensions={1} | all-to-all | bytes 204800 | tf_op jit(solution)/shard_map/all_to_all | solution.py:157
  458.3 7.1 %all-to-all-start.5 = ((bf16[16,5,8,1,80]{4,2,1,3,0:T(8,128)(2,1)}), bf16[16,5,8,1,80]{4,2,1,3,0:T(8,128)(2,1)S(1)}, u32[]{:S(2)}, u32[]{:S(2)}) async-start(bf16[16,5,8,1,80]{4,2,1,3,0:T(8,128)(2,1)} %bitcast.37), calls=%async_computation.5 | async-start | bytes 327680 | tf_op jit(solution)/shard_map/all_to_all | solution.py:156
  465.4 11.4 %copy.82 = bf16[8,16,80,256]{2,1,3,0:T(8,128)(2,1)} copy(bf16[8,16,80,256]{3,2,0,1:T(8,128)(2,1)} %bitcast.22) | data formatting | bytes 10485760 | tf_op jit(solution)/shard_map/reshape | solution.py:181
  476.8 14.0 %reshape_reshape.6 = bf16[8,1280,8,32]{1,3,2,0:T(8,128)(2,1)} reshape(bf16[8,16,80,256]{2,1,3,0:T(8,128)(2,1)} %copy.82) | data formatting | bytes 10485760 | tf_op jit(solution)/shard_map/reshape;reshape | solution.py:183
  491.1 1.3 broadcast_in_dim.69
  492.4 6.1 %all-to-all-start.6 = ((bf16[16,1,5,8,1280]{4,3,2,1,0:T(8,128)(2,1)}), bf16[16,1,5,8,1280]{4,3,2,1,0:T(8,128)(2,1)}, u32[]{:S(2)}, u32[]{:S(2)}) async-start(bf16[16,1,5,8,1280]{4,3,2,1,0:T(8,128)(2,1)} %broadcast_in_dim.69), calls=%async_computation.6 | async-start | bytes 3276800 | tf_op jit(solution)/shard_map/all_to_all | solution.py:18
  498.5 1.4 broadcast.152
  499.9 26.3 %while.34 = (s32[]{:T(128)}, bf16[10,8,80,128]{3,2,1,0:T(8,128)(2,1)}, bf16[10,8,80,128]{3,2,1,0:T(8,128)(2,1)S(1)}, bf16[10,8,80,128]{3,2,1,0:T(8,128)(2,1)}, b...) while((s32[]{:T(128)}, bf16[10,8,80,128]{3,2,1,0:T(8,128)(2,1)}, ...), condition=%wide.region_13.14_spmd, body=%wide.region_12.13_spmd.sunk | while | flops 253870080 | bytes 7110749 | solution.py:215
  526.2 10.8 %all-to-all-done.6 = bf16[16,1,5,8,1280]{4,3,2,1,0:T(8,128)(2,1)} async-done(((bf16[16,1,5,8,1280]{4,3,2,1,0:T(8,128)(2,1)}), bf16[16,1,5,8,1280]{4,3,2,1,0:T(8,128)(2,1)}, u32[]{:S(2)}, u32[]{:S(2)}) %all-to-all-start.6) | async-done | bytes 1638432 | tf_op jit(solution)/shard_map/all_to_all | solution.py:18
  536.9 4.5 fusion.29
  (200 shorter events, 71.8 us)
Async XLA Ops:
  7.2 535.9 %copy-start = (bf16[1,256,64]{1,2,0:T(8,128)(2,1)S(1)}, bf16[1,256,64]{1,2,0:T(8,128)(2,1)}, u32[]{:S(2)}) copy-start(bf16[1,256,64]{1,2,0:T(8,128)(2,1)} %param.25) | copy-start | bytes 98308
  7.2 181.0 %all-gather.2.cloned.1.call-start = ((), (), s32[]{:S(2)}) async-start(), calls=%async_computation.7 | async-start | bytes 11141120 | tf_op jit(solution)/shard_map/all_gather | solution.py:28
  59.7 5.7 %copy-start.1 = (bf16[128,80,32]{2,1,0:T(8,128)(2,1)S(1)}, bf16[128,80,32]{2,1,0:T(8,128)(2,1)}, u32[]{:S(2)}) copy-start(bf16[128,80,32]{2,1,0:T(8,128)(2,1)} %get-tuple-element.148) | copy-start | bytes 1966084
  189.3 1.0 copy-start.2
  267.7 1.4 copy-start.4
  267.7 1.4 copy-start.8
  286.8 19.2 %copy-start.6 = (bf16[1,64,512]{2,1,0:T(8,128)(2,1)S(1)}, bf16[1,64,512]{2,1,0:T(8,128)(2,1)}, u32[]{:S(2)}) copy-start(bf16[1,64,512]{2,1,0:T(8,128)(2,1)} %param.23) | copy-start | bytes 196612
  287.7 13.5 %all-to-all-start.2 = ((f32[16,80,8]{1,2,0:T(8,128)}), f32[16,80,8]{1,2,0:T(8,128)S(1)}, u32[]{:S(2)}, u32[]{:S(2)}) async-start(f32[16,80,8]{1,2,0:T(8,128)} %broadcast_in_dim.66), calls=%async_computation.2 | async-start | bytes 131072 | tf_op jit(solution)/shard_map/all_to_all | solution.py:18
  302.3 13.7 %all-to-all-start.3 = ((f32[16,80,8]{1,2,0:T(8,128)}), f32[16,80,8]{1,2,0:T(8,128)S(1)}, u32[]{:S(2)}, u32[]{:S(2)}) async-start(f32[16,80,8]{1,2,0:T(8,128)} %broadcast_in_dim.67), calls=%async_computation.3 | async-start | bytes 131072 | tf_op jit(solution)/shard_map/all_to_all | solution.py:18
  318.8 122.0 %all-to-all-start = ((bf16[16,8,80,256]{3,2,1,0:T(8,128)(2,1)}), bf16[16,8,80,256]{3,2,1,0:T(8,128)(2,1)}, u32[]{:S(2)}, u32[]{:S(2)}) async-start(bf16[16,8,80,256]{3,2,1,0:T(8,128)(2,1)} %stack.3), calls=%async_computation | async-start | bytes 10485760 | tf_op jit(solution)/shard_map/all_to_all | solution.py:180
  458.3 32.5 %all-to-all-start.5 = ((bf16[16,5,8,1,80]{4,2,1,3,0:T(8,128)(2,1)}), bf16[16,5,8,1,80]{4,2,1,3,0:T(8,128)(2,1)S(1)}, u32[]{:S(2)}, u32[]{:S(2)}) async-start(bf16[16,5,8,1,80]{4,2,1,3,0:T(8,128)(2,1)} %bitcast.37), calls=%async_computation.5 | async-start | bytes 327680 | tf_op jit(solution)/shard_map/all_to_all | solution.py:156
  492.4 44.6 %all-to-all-start.6 = ((bf16[16,1,5,8,1280]{4,3,2,1,0:T(8,128)(2,1)}), bf16[16,1,5,8,1280]{4,3,2,1,0:T(8,128)(2,1)}, u32[]{:S(2)}, u32[]{:S(2)}) async-start(bf16[16,1,5,8,1280]{4,3,2,1,0:T(8,128)(2,1)} %broadcast_in_dim.69), calls=%async_computation.6 | async-start | bytes 3276800 | tf_op jit(solution)/shard_map/all_to_all | solution.py:18
  498.5 1.4 copy-start.3
  498.5 1.4 copy-start.7
  542.6 0.9 copy-start.5
Sparse Core Ops, SparseCore 0:
  65.5 122.6 all-gather.1
